TPU v7x, 256 devices: a whole 4x4x8 slice. The times are simulated.
256 devices in a mesh: rep: 4 (over y), fsdp: 64 (over x, z, core).
Axes of the slice: x: 4, y: 4, z: 8, core: 2. Of those that a mesh axis runs over, the one named last changes fastest.
Arguments:
- grad_blocks: bfloat16 [4, 64, 512, 512], P('rep', None, 'fsdp'), may hold values from -6 to 6
- graft_accum: float32 [64, 512, 512], P(None, 'fsdp'), may hold values from 0.1 to 1000000
- left_stats: float32 [128, 512, 512], P('fsdp'), may hold values from -300000 to 300000, as said below
- right_stats: float32 [128, 512, 512], P('fsdp'), may hold values from -300000 to 300000, as said below
- block_slot: int32 [64], replicated, may hold values from 0 to 127, as said below
- vocab_grads: bfloat16 [4, 2, 512, 8192], P('rep', None, 'fsdp'), may hold values from -6 to 6
- vocab_accum: float32 [2, 512, 8192], P(None, 'fsdp'), may hold values from 0.01 to 10
Outputs:
- direction: bfloat16 [64, 512, 512], P(None, 'fsdp')
- graft_accum_new: float32 [64, 512, 512], P(None, 'fsdp')
- left_new: float32 [128, 512, 512], P('fsdp')
- right_new: float32 [128, 512, 512], P('fsdp')
- vocab_accum_new: float32 [2, 512, 8192], P(None, 'fsdp')
- vocab_step: bfloat16 [2, 512, 8192], P(None, 'fsdp')
Inputs may be any that keep to these rules, and one draw needn't show every extreme that they name: Block b's statistics sit in slot block_slot[b]; slot s belongs to fsdp index s // 2; no two blocks name the same slot; every fsdp index owns at most 2 blocks and some index owns exactly 2. `left_stats`: every slot holds a symmetric positive definite matrix. `right_stats`: every slot holds a symmetric positive definite matrix.
All inputs are finite; a program needn't handle non-finite values.
Results may differ from a plain program's by a relative error of at most 0.017.
Values may be sent and summed in bfloat16 or wider, within the bound.
A program may use at most 64 MiB of HBM per device.

v0:
```python
import jax
import jax.numpy as jnp
from jax import lax
from jax.sharding import PartitionSpec as P

ITERS = 6


def as_sent(shard):

    def short(part):
        return part.astype(jnp.bfloat16) if part.dtype == jnp.float32 else part

    return jax.tree.map(short, shard)


def batch_product(left, right):
    return jnp.einsum("sij,sjk->sik", left, right, precision=lax.Precision.HIGHEST)


def batch_root(matrices):
    matrix_order = matrices.shape[-1]
    identity = jnp.eye(matrix_order, dtype=jnp.float32)[None]
    frobenius = jnp.sqrt(jnp.sum(matrices * matrices, axis=(1, 2)))
    scaled = matrices / frobenius[:, None, None]
    result = identity
    for iteration in range(ITERS):
        factor = (5.0 * identity - scaled) * 0.25
        result = factor if iteration == 0 else batch_product(result, factor)
        if iteration + 1 < ITERS:
            square = batch_product(factor, factor)
            fourth = batch_product(square, square)
            scaled = batch_product(fourth, scaled)
    return result


def on_device(
    grad_blocks, graft_accum, left_stats, right_stats, block_slot, vocab_grads, vocab_accum
):
    summed_grad, summed_vocab = (
        lax.psum(grad_blocks[0].astype(jnp.float32).astype(jnp.bfloat16), "rep").astype(
            jnp.float32
        ),
        lax.psum(vocab_grads[0].astype(jnp.float32).astype(jnp.bfloat16), "rep").astype(
            jnp.float32
        ),
    )
    grad_sum = summed_grad.astype(jnp.bfloat16)
    vocab_sum = summed_vocab.astype(jnp.bfloat16)
    vocab_float = vocab_sum.astype(jnp.float32)
    vocab_accum_new = vocab_accum + vocab_float * vocab_float
    vocab_step = (vocab_float / (jnp.sqrt(vocab_accum_new) + 1e-10)).astype(jnp.bfloat16)
    grad_float = grad_sum.astype(jnp.float32)
    graft_accum_new = graft_accum + grad_float * grad_float
    grafted = grad_float / (jnp.sqrt(graft_accum_new) + 1e-10)
    graft_part = jnp.sum(grafted * grafted, axis=(1, 2))
    matrix_order = grad_blocks.shape[-1]
    entries = float(matrix_order * matrix_order)
    slot_count = left_stats.shape[0]
    total_slots = slot_count * lax.axis_size("fsdp")
    onehot = (block_slot[None, :] == jnp.arange(total_slots, dtype=jnp.int32)[:, None]).astype(
        jnp.bfloat16
    )
    outgoing = jnp.einsum(
        "sb,brc->src", onehot, grad_sum, preferred_element_type=jnp.float32
    ).astype(jnp.bfloat16)
    received = lax.all_to_all(outgoing, "fsdp", split_axis=0, concat_axis=1, tiled=True)
    left_new = left_stats + jnp.einsum(
        "sij,skj->sik", received, received, preferred_element_type=jnp.float32
    )
    right_new = right_stats + jnp.einsum(
        "sji,sjk->sik", received, received, preferred_element_type=jnp.float32
    )
    stacked = jnp.concatenate([left_new, right_new], axis=0)
    share_count = stacked.shape[0] // lax.axis_size("rep")
    own_share = lax.dynamic_slice_in_dim(
        stacked, lax.axis_index("rep") * share_count, share_count, 0
    )
    inverse_roots = lax.all_gather(
        batch_root(own_share).astype(jnp.bfloat16), "rep", axis=0, tiled=True
    ).astype(jnp.float32)
    block_float = received.astype(jnp.float32)
    shampoo = batch_product(
        batch_product(inverse_roots[:slot_count], block_float), inverse_roots[slot_count:]
    )
    returned = lax.all_to_all(
        as_sent(shampoo), "fsdp", split_axis=1, concat_axis=0, tiled=True
    ).astype(shampoo.dtype)
    shampoo_rows = jnp.take(returned, block_slot, axis=0)
    shampoo_part = jnp.sum(shampoo_rows * shampoo_rows, axis=(1, 2))
    graft_total, shampoo_total = lax.psum((graft_part, shampoo_part), "fsdp")
    graft_scale = jnp.sqrt(graft_total / entries) / jnp.sqrt(shampoo_total / entries + 1e-06)
    direction = (shampoo_rows * graft_scale[:, None, None]).astype(jnp.bfloat16)
    return (direction, graft_accum_new, left_new, right_new, vocab_accum_new, vocab_step)


def solution(mesh):
    in_specs = (
        P("rep", None, "fsdp", None),
        P(None, "fsdp", None),
        P("fsdp", None, None),
        P("fsdp", None, None),
        P(),
        P("rep", None, "fsdp", None),
        P(None, "fsdp", None),
    )
    out_specs = (
        P(None, "fsdp", None),
        P(None, "fsdp", None),
        P("fsdp", None, None),
        P("fsdp", None, None),
        P(None, "fsdp", None),
        P(None, "fsdp", None),
    )
    return jax.shard_map(
        on_device, mesh=mesh, in_specs=in_specs, out_specs=out_specs, check_vma=False
    )
```

profile of v0, /device:TPU:8, one launch (start us, length us, event | category | flops | bytes accessed | tf_op | source)
XLA Modules:
  0.0 361.6 jit_solution(7396740100654670768)
XLA Ops:
  7.2 2.0 copy.57
  9.2 53.5 %all-reduce.4.cloned.1.call-done = (bf16[64,8,512]{2,0,1:T(8,128)(2,1)}, bf16[2,8,8192]{2,1,0:T(8,128)(2,1)}) async-done(((bf16[64,8,512]{2,0,1:T(8,128)(2,1)}, bf16[2,8,8192]{2,1,0:T(8,128)(2,1)}), (bf16[64,8,512]{2,0,1:T(8,128)(2,1)}, bf16[2,8,8192]{2,1,0:T(8,128)(2,1)})) %all-reduce.4.cloned.1.call-update) | async-done | bytes 786448 | tf_op jit(solution)/shard_map/psum | solution.py:41
  65.9 10.4 %all-to-all-start = ((bf16[128,8,512]{2,1,0:T(8,128)(2,1)}), bf16[128,8,512]{2,1,0:T(8,128)(2,1)S(1)}, u32[]{:S(2)}, u32[]{:S(2)}) async-start(bf16[128,8,512]{2,1,0:T(8,128)(2,1)} %copy.32), calls=%async_computation | async-start | bytes 2097152 | tf_op jit(solution)/shard_map/all_to_all | solution.py:67
  77.0 27.6 %all-to-all-done = bf16[128,8,512]{2,1,0:T(8,128)(2,1)S(1)} async-done(((bf16[128,8,512]{2,1,0:T(8,128)(2,1)}), bf16[128,8,512]{2,1,0:T(8,128)(2,1)S(1)}, u32[]{:S(2)}, u32[]{:S(2)}) %all-to-all-start) | async-done | bytes 1048608 | tf_op jit(solution)/shard_map/all_to_all | solution.py:67
  104.5 2.5 convolution_add_fusion
  112.2 1.9 fusion.12
  114.1 1.8 fusion.102
  116.0 1.8 fusion.8
  117.8 2.0 fusion.10
  119.8 1.9 fusion.31
  121.7 1.8 fusion.103
  123.6 2.0 fusion.104
  125.6 1.9 fusion.27
  127.5 1.9 fusion.29
  129.5 1.8 fusion.105
  131.3 1.8 fusion.106
  133.2 1.9 fusion.23
  135.1 1.9 fusion.25
  137.0 2.1 fusion.107
  139.1 1.8 fusion.108
  140.9 1.9 fusion.19
  142.9 1.9 fusion.21
  144.8 1.8 fusion.109
  146.6 1.9 fusion
  148.5 2.6 convolution_convert_fusion.2
  151.2 29.0 %all-gather.3.cloned.1.call-done = bf16[2048,512]{1,0:T(8,128)(2,1)} async-done(((bf16[512,512]{1,0:T(8,128)(2,1)}), bf16[2048,512]{1,0:T(8,128)(2,1)}) %all-gather.3.cloned.1.call-update) | async-done | bytes 2097168 | tf_op jit(solution)/shard_map/all_gather | solution.py:79
  180.2 1.7 fusion.101
  182.6 2.1 convolution_convert_fusion.1
  184.7 2.0 copy.35
  186.8 10.4 %all-to-all-start.1 = ((bf16[2,512,512]{2,0,1:T(2,128)(2,1)}), bf16[2,512,512]{2,0,1:T(2,128)(2,1)S(1)}, u32[]{:S(2)}, u32[]{:S(2)}) async-start(bf16[2,512,512]{2,0,1:T(2,128)(2,1)} %copy.35), calls=%async_computation.1 | async-start | bytes 2097152 | tf_op jit(solution)/shard_map/all_to_all | solution.py:86
  200.8 24.6 %all-to-all-done.1 = bf16[2,512,512]{2,0,1:T(2,128)(2,1)S(1)} async-done(((bf16[2,512,512]{2,0,1:T(2,128)(2,1)}), bf16[2,512,512]{2,0,1:T(2,128)(2,1)S(1)}, u32[]{:S(2)}, u32[]{:S(2)}) %all-to-all-start.1) | async-done | bytes 1048608 | tf_op jit(solution)/shard_map/all_to_all | solution.py:86
  227.5 126.0 %all-reduce = (f32[64]{0:T(128)S(1)}, f32[64]{0:T(128)S(1)}) all-reduce(f32[64]{0:T(128)S(1)} %multiply_reduce_fusion, f32[64]{0:T(128)S(1)} %get-tuple-element.36), channel_id=1, replica_groups=mesh['rep'=4,'fsdp'=64] {'fsdp'}, use_global_device_ids=true, to_apply=%region_5.6 | all-reduce | flops 128 | bytes 1024 | tf_op jit(solution)/shard_map/psum | solution.py:91
  (38 shorter events, 15.6 us)
Async XLA Ops:
  7.2 55.6 %all-reduce.4.cloned.1.call-start = ((), (), s32[]{:S(2)}) async-start(), calls=%async_computation.3 | async-start | bytes 1572864 | tf_op jit(solution)/shard_map/psum | solution.py:41
  65.9 38.6 %all-to-all-start = ((bf16[128,8,512]{2,1,0:T(8,128)(2,1)}), bf16[128,8,512]{2,1,0:T(8,128)(2,1)S(1)}, u32[]{:S(2)}, u32[]{:S(2)}) async-start(bf16[128,8,512]{2,1,0:T(8,128)(2,1)} %copy.32), calls=%async_computation | async-start | bytes 2097152 | tf_op jit(solution)/shard_map/all_to_all | solution.py:67
  76.4 103.9 %all-gather.3.cloned.1.call-start = ((), (), s32[]{:S(2)}) async-start(), calls=%async_computation.2 | async-start | bytes 2621440 | tf_op jit(solution)/shard_map/all_gather | solution.py:79
  104.5 2.5 copy-start.2
  107.0 3.7 %copy-start = (f32[2,512,512]{2,1,0:T(8,128)}, f32[2,512,512]{2,1,0:T(8,128)S(1)}, u32[]{:S(2)}) copy-start(f32[2,512,512]{2,1,0:T(8,128)S(1)} %convolution_add_fusion) | copy-start | bytes 6291460
  107.8 1.3 copy-start.1
  148.5 2.7 copy-start.7
  184.7 12.5 %copy-start.3 = (bf16[64,8,512]{2,0,1:T(8,128)(2,1)S(1)}, bf16[64,8,512]{2,0,1:T(8,128)(2,1)}, u32[]{:S(2)}) copy-start(bf16[64,8,512]{2,0,1:T(8,128)(2,1)} %get-tuple-element.32) | copy-start | bytes 1572868
  184.7 12.5 %copy-start.4 = (f32[64,8,512]{2,1,0:T(8,128)S(1)}, f32[64,8,512]{2,1,0:T(8,128)}, u32[]{:S(2)}) copy-start(f32[64,8,512]{2,1,0:T(8,128)} %param.8) | copy-start | bytes 3145732
  186.8 38.6 %all-to-all-start.1 = ((bf16[2,512,512]{2,0,1:T(2,128)(2,1)}), bf16[2,512,512]{2,0,1:T(2,128)(2,1)S(1)}, u32[]{:S(2)}, u32[]{:S(2)}) async-start(bf16[2,512,512]{2,0,1:T(2,128)(2,1)} %copy.35), calls=%async_computation.1 | async-start | bytes 2097152 | tf_op jit(solution)/shard_map/all_to_all | solution.py:86
  197.2 2.5 copy-start.5
  197.3 2.5 copy-start.6
Sparse Core Ops, SparseCore 0:
  11.0 51.6 all-reduce.3
  151.3 28.9 all-gather.2
where the time goes:
time: 364 us; the launch traced here: 362 us
  waiting for transfers between devices  135 us (37%)
  blocking collectives  126 us (35%)
  matrix products  46.4 us (13%)
  starting transfers between devices  21.5 us (6%)
  between operations  15.4 us (4%)
  local copies, waits for them, and re-layouts  11 us (3%)
  other arithmetic  6.57 us (2%)
    psum x1, blocking collectives, on_device(): graft_total, shampoo_total = lax.psum((graft_part, shampoo_part), 'fsdp')  126 us
    psum x1, waiting for transfers between devices, on_device(): lax.psum(grad_blocks[0].astype(jnp.float32).astype(jnp.bfloat16), 'rep')  53.5 us
    dot_general x22, matrix products, batch_product(): jnp.einsum('sij,sjk->sik', left, right, precision=lax.Precision.HIGHEST)  41.6 us
    all_gather x1, waiting for transfers between devices, on_device(): lax.all_gather(batch_root(own_share).astype(jnp.bfloat16), 'rep', axis=0,...  29 us
    all_to_all x1, waiting for transfers between devices, on_device(): lax.all_to_all(outgoing, 'fsdp', split_axis=0, concat_axis=1, tiled=True)  27.6 us
    all_to_all x1, waiting for transfers between devices, on_device(): lax.all_to_all(as_sent(shampoo), 'fsdp', split_axis=1, concat_axis=0, til...  24.6 us
    all_to_all x1, starting transfers between devices, on_device(): lax.all_to_all(as_sent(shampoo), 'fsdp', split_axis=1, concat_axis=0, til...  10.4 us
    all_to_all x1, starting transfers between devices, on_device(): lax.all_to_all(outgoing, 'fsdp', split_axis=0, concat_axis=1, tiled=True)  10.4 us
  transfers between devices with their start and end apart: 4, of which 4 were waited for; matrix products, arithmetic and copies ran while one was open for 1% of the time, Pallas kernels for 0%

commit v1 on v0

--- a/solution.py
+++ b/solution.py
@@ -1,9 +1,22 @@
+import functools
 import jax
 import jax.numpy as jnp
 from jax import lax
 from jax.sharding import PartitionSpec as P
 
 ITERS = 6
+
+
+def turns_part(vec, link_axis):
+    near = jax.lax.psum(1, link_axis)
+    extra = jnp.split(vec, near, 1)
+    t1 = jnp.stack(extra, 0)
+    val2 = jax.lax.all_to_all(t1, link_axis, 0, 0)
+    outcome_arr = jnp.concatenate(val2, 0)
+    return outcome_arr
+
+
+field_treat = functools.partial(turns_part, link_axis="fsdp")
 
 
 def as_sent(shard):
@@ -83,9 +96,7 @@
     shampoo = batch_product(
         batch_product(inverse_roots[:slot_count], block_float), inverse_roots[slot_count:]
     )
-    returned = lax.all_to_all(
-        as_sent(shampoo), "fsdp", split_axis=1, concat_axis=0, tiled=True
-    ).astype(shampoo.dtype)
+    returned = field_treat(as_sent(shampoo)).astype(shampoo.dtype)
     shampoo_rows = jnp.take(returned, block_slot, axis=0)
     shampoo_part = jnp.sum(shampoo_rows * shampoo_rows, axis=(1, 2))
     graft_total, shampoo_total = lax.psum((graft_part, shampoo_part), "fsdp")

time: 364 us -> 401 us (1.10)
  local copies, waits for them, and re-layouts: 11 us -> 47.2 us
    unnamed x18 -> x81, local copies, waits for them, and re-layouts: 4.93 us -> 42.8 us
where the time goes in v1:
time: 401 us; the launch traced here: 398 us
  waiting for transfers between devices  135 us (34%)
  blocking collectives  126 us (31%)
  local copies, waits for them, and re-layouts  47.2 us (12%)
  matrix products  46.4 us (12%)
  starting transfers between devices  21.5 us (5%)
  between operations  15.4 us (4%)
  other arithmetic  6.66 us (2%)
    psum x1, blocking collectives, on_device(): graft_total, shampoo_total = lax.psum((graft_part, shampoo_part), 'fsdp')  126 us
    psum x1, waiting for transfers between devices, on_device(): lax.psum(grad_blocks[0].astype(jnp.float32).astype(jnp.bfloat16), 'rep')  53.5 us
    unnamed x81, local copies, waits for them, and re-layouts  42.8 us
    dot_general x22, matrix products, batch_product(): jnp.einsum('sij,sjk->sik', left, right, precision=lax.Precision.HIGHEST)  41.6 us
    all_gather x1, waiting for transfers between devices, on_device(): lax.all_gather(batch_root(own_share).astype(jnp.bfloat16), 'rep', axis=0,...  29 us
    all_to_all x1, waiting for transfers between devices, on_device(): lax.all_to_all(outgoing, 'fsdp', split_axis=0, concat_axis=1, tiled=True)  27.6 us
    all_to_all x1, waiting for transfers between devices, turns_part(): val2 = jax.lax.all_to_all(t1, link_axis, 0, 0)  24.6 us
    all_to_all x1, starting transfers between devices, turns_part(): val2 = jax.lax.all_to_all(t1, link_axis, 0, 0)  10.4 us
  transfers between devices with their start and end apart: 4, of which 4 were waited for; matrix products, arithmetic and copies ran while one was open for 1% of the time, Pallas kernels for 0%

profile of v1, /device:TPU:8, one launch (start us, length us, event | category | flops | bytes accessed | tf_op | source)
XLA Modules:
  0.0 397.9 jit_solution(11093587800116326034)
XLA Ops:
  7.2 2.0 copy.45
  9.2 53.5 %all-reduce.4.cloned.1.call-done = (bf16[64,8,512]{2,0,1:T(8,128)(2,1)}, bf16[2,8,8192]{2,1,0:T(8,128)(2,1)}) async-done(((bf16[64,8,512]{2,0,1:T(8,128)(2,1)}, bf16[2,8,8192]{2,1,0:T(8,128)(2,1)}), (bf16[64,8,512]{2,0,1:T(8,128)(2,1)}, bf16[2,8,8192]{2,1,0:T(8,128)(2,1)})) %all-reduce.4.cloned.1.call-update) | async-done | bytes 786448 | tf_op jit(solution)/shard_map/psum | solution.py:54
  62.8 1.6 convolution_convert_fusion
  65.9 10.4 %all-to-all-start = ((bf16[128,8,512]{2,1,0:T(8,128)(2,1)}), bf16[128,8,512]{2,1,0:T(8,128)(2,1)S(1)}, u32[]{:S(2)}, u32[]{:S(2)}) async-start(bf16[128,8,512]{2,1,0:T(8,128)(2,1)} %copy.24), calls=%async_computation | async-start | bytes 2097152 | tf_op jit(solution)/shard_map/all_to_all | solution.py:80
  77.0 27.6 %all-to-all-done = bf16[128,8,512]{2,1,0:T(8,128)(2,1)S(1)} async-done(((bf16[128,8,512]{2,1,0:T(8,128)(2,1)}), bf16[128,8,512]{2,1,0:T(8,128)(2,1)S(1)}, u32[]{:S(2)}, u32[]{:S(2)}) %all-to-all-start) | async-done | bytes 1048608 | tf_op jit(solution)/shard_map/all_to_all | solution.py:80
  104.5 2.5 convolution_add_fusion
  112.2 1.9 fusion.12
  114.1 1.8 fusion.102
  116.0 1.8 fusion.8
  117.8 2.0 fusion.10
  119.8 1.9 fusion.31
  121.7 1.8 fusion.103
  123.6 2.0 fusion.104
  125.6 1.9 fusion.27
  127.5 1.9 fusion.29
  129.5 1.8 fusion.105
  131.3 1.8 fusion.106
  133.2 1.9 fusion.23
  135.1 1.9 fusion.25
  137.0 2.1 fusion.107
  139.1 1.8 fusion.108
  140.9 1.9 fusion.19
  142.9 1.9 fusion.21
  144.8 1.8 fusion.109
  146.6 1.9 fusion
  148.5 2.6 convolution_convert_fusion.2
  151.2 29.0 %all-gather.3.cloned.1.call-done = bf16[2048,512]{1,0:T(8,128)(2,1)} async-done(((bf16[512,512]{1,0:T(8,128)(2,1)}), bf16[2048,512]{1,0:T(8,128)(2,1)}) %all-gather.3.cloned.1.call-update) | async-done | bytes 2097168 | tf_op jit(solution)/shard_map/all_gather | solution.py:92
  180.2 1.7 fusion.101
  182.6 2.1 convolution_convert_fusion.1
  223.2 10.4 %all-to-all-start.1 = ((bf16[64,2,8,512]{3,2,1,0:T(8,128)(2,1)}), bf16[64,2,8,512]{3,2,1,0:T(8,128)(2,1)S(1)}, u32[]{:S(2)}, u32[]{:S(2)}) async-start(bf16[64,2,8,512]{3,2,1,0:T(8,128)(2,1)} %constant_dynamic-update-slice_fusion), calls=%async_computation.1 | async-start | bytes 2097152 | tf_op jit(solution)/shard_map/all_to_all | solution.py:14
  237.2 24.6 %all-to-all-done.1 = bf16[64,2,8,512]{3,2,1,0:T(8,128)(2,1)S(1)} async-done(((bf16[64,2,8,512]{3,2,1,0:T(8,128)(2,1)}), bf16[64,2,8,512]{3,2,1,0:T(8,128)(2,1)S(1)}, u32[]{:S(2)}, u32[]{:S(2)}) %all-to-all-start.1) | async-done | bytes 1048608 | tf_op jit(solution)/shard_map/all_to_all | solution.py:14
  263.8 126.0 %all-reduce = (f32[64]{0:T(128)S(1)}, f32[64]{0:T(128)S(1)}) all-reduce(f32[64]{0:T(128)S(1)} %multiply_reduce_fusion, f32[64]{0:T(128)S(1)} %get-tuple-element.30), channel_id=1, replica_groups=mesh['rep'=4,'fsdp'=64] {'fsdp'}, use_global_device_ids=true, to_apply=%region_5.6 | all-reduce | flops 128 | bytes 1024 | tf_op jit(solution)/shard_map/psum | solution.py:102
  (100 shorter events, 52.3 us)
Async XLA Ops:
  7.2 55.6 %all-reduce.4.cloned.1.call-start = ((), (), s32[]{:S(2)}) async-start(), calls=%async_computation.3 | async-start | bytes 1572864 | tf_op jit(solution)/shard_map/psum | solution.py:54
  65.9 38.6 %all-to-all-start = ((bf16[128,8,512]{2,1,0:T(8,128)(2,1)}), bf16[128,8,512]{2,1,0:T(8,128)(2,1)S(1)}, u32[]{:S(2)}, u32[]{:S(2)}) async-start(bf16[128,8,512]{2,1,0:T(8,128)(2,1)} %copy.24), calls=%async_computation | async-start | bytes 2097152 | tf_op jit(solution)/shard_map/all_to_all | solution.py:80
  76.4 103.9 %all-gather.3.cloned.1.call-start = ((), (), s32[]{:S(2)}) async-start(), calls=%async_computation.2 | async-start | bytes 2621440 | tf_op jit(solution)/shard_map/all_gather | solution.py:92
  104.5 2.5 copy-start.2
  107.0 3.7 copy-start
  107.8 1.3 copy-start.1
  148.5 2.7 copy-start.7
  184.7 48.9 %copy-start.3 = (bf16[64,8,512]{2,0,1:T(8,128)(2,1)S(1)}, bf16[64,8,512]{2,0,1:T(8,128)(2,1)}, u32[]{:S(2)}) copy-start(bf16[64,8,512]{2,0,1:T(8,128)(2,1)} %get-tuple-element.26) | copy-start | bytes 1572868
  184.7 48.9 %copy-start.4 = (f32[64,8,512]{2,1,0:T(8,128)S(1)}, f32[64,8,512]{2,1,0:T(8,128)}, u32[]{:S(2)}) copy-start(f32[64,8,512]{2,1,0:T(8,128)} %param.8) | copy-start | bytes 3145732
  223.2 38.6 %all-to-all-start.1 = ((bf16[64,2,8,512]{3,2,1,0:T(8,128)(2,1)}), bf16[64,2,8,512]{3,2,1,0:T(8,128)(2,1)S(1)}, u32[]{:S(2)}, u32[]{:S(2)}) async-start(bf16[64,2,8,512]{3,2,1,0:T(8,128)(2,1)} %constant_dynamic-update-slice_fusion), calls=%async_computation.1 | async-start | bytes 2097152 | tf_op jit(solution)/shard_map/all_to_all | solution.py:14
  233.7 2.5 copy-start.5
  233.7 2.5 copy-start.6
Sparse Core Ops, SparseCore 0:
  11.0 51.6 all-reduce.3
  151.3 28.9 all-gather.2
